TPU v7x, 32 devices: a whole 2x2x4 slice. The times are simulated.
32 devices in a mesh: gx: 2 (over x), gy: 4 (over z), gz: 4 (over y, core).
Axes of the slice: x: 2, y: 2, z: 4, core: 2. Of those that a mesh axis runs over, the one named last changes fastest.
Arguments:
- local_displacement: float32 [2, 4, 4, 6, 128, 128], P('gx', 'gy', 'gz'), may hold values from -6 to 6
- coarse_load: float32 [2, 4, 4, 6, 128], P('gx', 'gy', 'gz'), may hold values from -12 to 12
- flexibility: float32 [2, 4, 4, 768, 768], P('gx', 'gy', 'gz'), as said below
- block_map: int32 [2, 4, 4, 768], P('gx', 'gy', 'gz'), may hold values from 0 to 767, each once within a row
- mode_counts: int32 [2, 4, 4], P('gx', 'gy', 'gz'), may hold values from 3 to 6, as said below
- mode_traces: float32 [2, 4, 4, 6, 6, 128], P('gx', 'gy', 'gz')
- coarse_rows: float32 [2, 4, 4, 6, 192], P('gx', 'gy', 'gz'), as said below
- stored_dirs: float32 [2, 4, 4, 40, 6, 128], P('gx', 'gy', 'gz'), as said below
- stored_images: float32 [2, 4, 4, 40, 6, 128], P('gx', 'gy', 'gz'), as said below
- stored_curv: float32 [40], replicated, may hold values from 1 to 4
Outputs:
- multipliers: float32 [2, 4, 4, 6, 128, 128], P('gx', 'gy', 'gz')
- residual: float32 [2, 4, 4, 6, 128, 128], P('gx', 'gy', 'gz')
Inputs may be any that keep to these rules, and one draw needn't show every extreme that they name: `flexibility`: each subdomain's matrix is symmetric positive definite. `coarse_rows`: read as a [192, 192] matrix it is exactly symmetric: the inverse of G^T G for the coarse basis G of the present modes, with ones added on the diagonal of absent modes. `mode_counts`: modes numbered from the count on are absent. `block_map`: each subdomain's row names every interface position once. `stored_dirs`: both copies of every face agree: slot 2a of a subdomain equals slot 2a+1 of its lower neighbour along grid dimension a. `stored_images`: both copies of every face agree: slot 2a of a subdomain equals slot 2a+1 of its lower neighbour along grid dimension a.
All inputs are finite; a program needn't handle non-finite values.
Results may differ from a plain program's by a relative error of at most 0.0003.
Values sent between devices are 32-bit elements; how exact they have to be, the bound alone decides.
A program may use at most 128 MiB of HBM per device.

v0:
```python
import jax
import jax.numpy as jnp
from jax import lax
from jax.sharding import PartitionSpec as P

STORED = 40
ITERS = 3
precise = lax.Precision.HIGHEST
slot_signs = (-1.0, 1.0, -1.0, 1.0, -1.0, 1.0)


def extended(x, sides, width):
    for axis, dim in sides:
        peers, length = (lax.axis_size(axis), x.shape[dim])
        up = [(i, (i + 1) % peers) for i in range(peers)]
        down = [(j, i) for i, j in up]
        last = lax.slice_in_dim(x, length - width, length, axis=dim)
        initial = lax.slice_in_dim(x, 0, width, axis=dim)
        before = lax.ppermute(last, axis, up)
        after = lax.ppermute(initial, axis, down)
        x = jnp.concatenate([before, x, after], axis=dim)
    return x


def assemble(field):
    padded_x = extended(field[0:2], (("gx", 0),), 1)
    padded_y = extended(field[2:4], (("gy", 0),), 1)
    padded_z = extended(field[4:6], (("gz", 0),), 1)
    return jnp.stack(
        [
            field[0] + padded_x[0],
            field[1] + padded_x[3],
            field[2] + padded_y[0],
            field[3] + padded_y[3],
            field[4] + padded_z[0],
            field[5] + padded_z[3],
        ]
    )


def plus_inner(first, second):
    return jnp.sum(first[1::2] * second[1::2], axis=(0, 1))


def stored_inner(store, field):
    return jnp.einsum("isf,sfr->ir", store[:, 1::2], field[1::2], precision=precise)


def coarse_solve(loads, rows):
    return jnp.dot(
        rows, lax.all_gather(loads, ("gx", "gy", "gz"), axis=0, tiled=True), precision=precise
    )


def per_device(
    local_displacement,
    coarse_load,
    flexibility,
    block_map,
    mode_counts,
    mode_traces,
    coarse_rows,
    stored_dirs,
    stored_images,
    stored_curv,
):
    displacement = local_displacement[0, 0, 0]
    loads = coarse_load[0, 0, 0]
    flex = flexibility[0, 0, 0]
    mapping = block_map[0, 0, 0]
    rows = coarse_rows[0, 0, 0]
    dirs_store = stored_dirs[0, 0, 0]
    images_store = stored_images[0, 0, 0]
    signs = jnp.array(slot_signs, jnp.float32)
    field_signs = signs[:, None, None]
    nmodes = mode_traces.shape[3]
    present = (jnp.arange(nmodes, dtype=jnp.int32) < mode_counts[0, 0, 0]).astype(jnp.float32)
    signed = mode_traces[0, 0, 0] * present[:, None, None] * signs[None, :, None]
    size_nb = flex.shape[0]
    inverse = jnp.zeros((size_nb,), jnp.int32).at[mapping].set(jnp.arange(size_nb, dtype=jnp.int32))
    flex_face = jnp.take(jnp.take(flex, inverse, axis=0), inverse, axis=1)
    layout = displacement.shape

    def operate(field):
        flat = (field_signs * field).reshape(size_nb, layout[2])
        return jnp.dot(flex_face, flat, precision=precise).reshape(layout)

    def graph(alpha):
        return assemble(jnp.einsum("msf,mr->sfr", signed, alpha, precision=precise))

    def project(field):
        partial_loads = jnp.einsum("msf,sfr->mr", signed, field, precision=precise)
        return field - graph(coarse_solve(partial_loads, rows))

    lam = graph(coarse_solve(loads, rows))
    resid = project(assemble(field_signs * (displacement - operate(lam))))
    directions, images, curves = ([], [], [])
    for step in range(ITERS):
        local_rows = stored_inner(images_store, resid)
        if images:
            own_rows = jnp.stack([plus_inner(images[index], resid) for index in range(len(images))])
            local_rows = jnp.concatenate([local_rows, own_rows], axis=0)
        totals = lax.psum(local_rows, ("gx", "gy", "gz"))
        beta = totals[:STORED] / stored_curv[:, None]
        direction = resid - jnp.einsum("isf,ir->sfr", dirs_store, beta, precision=precise)
        for index in range(len(directions)):
            direction = direction - directions[index] * (totals[STORED + index] / curves[index])
        image_now = project(assemble(field_signs * operate(direction)))
        pair = lax.psum(
            jnp.stack([plus_inner(direction, image_now), plus_inner(direction, resid)]),
            ("gx", "gy", "gz"),
        )
        rate = pair[1] / pair[0]
        lam = lam + rate * direction
        resid = resid - rate * image_now
        directions.append(direction)
        images.append(image_now)
        curves.append(pair[0])
    return (lam[None, None, None], resid[None, None, None])


def solution(mesh):
    return jax.shard_map(
        per_device,
        mesh=mesh,
        in_specs=(
            P("gx", "gy", "gz", None, None, None),
            P("gx", "gy", "gz", None, None),
            P("gx", "gy", "gz", None, None),
            P("gx", "gy", "gz", None),
            P("gx", "gy", "gz"),
            P("gx", "gy", "gz", None, None, None),
            P("gx", "gy", "gz", None, None),
            P("gx", "gy", "gz", None, None, None),
            P("gx", "gy", "gz", None, None, None),
            P(),
        ),
        out_specs=(P("gx", "gy", "gz", None, None, None), P("gx", "gy", "gz", None, None, None)),
        check_vma=False,
    )
```

profile of v0, /device:TPU:10, one launch (start us, length us, event | category | flops | bytes accessed | tf_op | source)
XLA Modules:
  0.0 665.6 jit_solution(9631356648595068276)
XLA Ops:
  1.5 37.6 %all-gather = f32[1,1,1,192,128]{4,2,1,0,3:T(1,128)S(1)} all-gather(f32[1,1,1,6,128]{4,2,1,0,3:T(1,128)} %bitcast.275), channel_id=2, replica_groups=mesh['gx'=2,'gy'=4,'gz'=4] {'gx','gy','gz'}, dimensions={3}, use_global_device_ids=true | all-gather | bytes 101376 | tf_op jit(solution)/shard_map/all_gather | solution.py:51
  41.6 1.6 collective-permute-start
  43.9 3.4 scatter_custom_fusion
  47.3 3.5 gather_fusion
  50.8 3.3 broadcast_select_fusion
  54.1 3.0 copy.40
  57.1 5.8 gather_fusion.1
  64.3 3.3 select_bitcast_fusion
  67.7 3.1 copy.41
  71.2 4.2 collective-permute-start.3
  76.3 1.8 collective-permute-done.2
  78.9 3.7 fusion.4
  82.6 1.6 collective-permute-start.6
  84.2 2.8 collective-permute-done.6
  87.5 4.6 collective-permute-start.8
  94.2 2.1 collective-permute-done.7
  96.4 1.6 collective-permute-done.9
  99.1 37.6 %all-gather.1 = f32[32,6,128]{2,1,0:T(8,128)S(1)} all-gather(f32[1,6,128]{2,1,0:T(8,128)S(1)} %convolution_bitcast_fusion.14), channel_id=1, replica_groups=mesh['gx'=2,'gy'=4,'gz'=4] {'gx','gy','gz'}, dimensions={0}, use_global_device_ids=true | all-gather | bytes 101376 | tf_op jit(solution)/shard_map/all_gather | solution.py:51
  142.8 4.2 collective-permute-start.15
  148.4 3.0 collective-permute-done.13
  153.1 43.5 %psum.42 = f32[40,128]{1,0:T(8,128)} all-reduce(f32[40,128]{1,0:T(8,128)S(1)} %convolution_bitcast_fusion.5), channel_id=1, replica_groups=mesh['gx'=2,'gy'=4,'gz'=4] {'gx','gy','gz'}, use_global_device_ids=true, to_apply=%region_1.2 | all-reduce | flops 5120 | bytes 40960 | tf_op jit(solution)/shard_map/psum | solution.py:103
  196.6 1.8 broadcast_multiply_fusion.2
  198.4 3.7 convolution_multiply_fusion.2
  202.4 4.1 collective-permute-done.18
  209.7 3.6 collective-permute-done.19
  214.1 39.5 %all-gather.2 = f32[32,6,128]{2,1,0:T(8,128)} all-gather(f32[1,6,128]{2,1,0:T(8,128)S(1)} %convolution_bitcast_fusion.13), channel_id=1, replica_groups=mesh['gx'=2,'gy'=4,'gz'=4] {'gx','gy','gz'}, dimensions={0}, use_global_device_ids=true | all-gather | bytes 101376 | tf_op jit(solution)/shard_map/all_gather | solution.py:51
  253.6 1.6 reshape.910
  256.2 1.6 fusion.30
  259.0 1.5 constant_dynamic-update-slice_fusion.70
  260.5 1.5 constant_dynamic-update-slice_fusion.69
  262.0 1.5 constant_dynamic-update-slice_fusion.68
  263.5 1.5 constant_dynamic-update-slice_fusion.67
  265.0 1.5 constant_dynamic-update-slice_fusion.66
  267.2 4.2 collective-permute-start.27
  272.8 3.4 collective-permute-done.25
  278.5 42.5 %psum.43 = f32[2,128]{1,0:T(2,128)S(1)} all-reduce(f32[2,128]{1,0:T(2,128)S(1)} %pad_maximum_fusion.2), channel_id=1, replica_groups=mesh['gx'=2,'gy'=4,'gz'=4] {'gx','gy','gz'}, use_global_device_ids=true, to_apply=%region_4.5 | all-reduce | flops 256 | bytes 2048 | tf_op jit(solution)/shard_map/psum | solution.py:109
  324.6 39.2 %psum.44 = f32[41,128]{1,0:T(8,128)S(1)} all-reduce(f32[41,128]{1,0:T(8,128)S(1)} %pad_maximum_fusion), channel_id=1, replica_groups=mesh['gx'=2,'gy'=4,'gz'=4] {'gx','gy','gz'}, use_global_device_ids=true, to_apply=%region_6.7 | all-reduce | flops 5248 | bytes 41984 | tf_op jit(solution)/shard_map/psum | solution.py:103
  364.5 2.6 broadcast_multiply_fusion.1
  367.1 3.7 convolution_multiply_fusion.1
  371.0 4.1 collective-permute-done.30
  378.5 3.9 collective-permute-done.31
  383.3 38.7 %all-gather.3 = f32[32,6,128]{2,1,0:T(8,128)S(1)} all-gather(f32[1,6,128]{2,1,0:T(8,128)S(1)} %convolution_bitcast_fusion.12), channel_id=1, replica_groups=mesh['gx'=2,'gy'=4,'gz'=4] {'gx','gy','gz'}, dimensions={0}, use_global_device_ids=true | all-gather | bytes 101376 | tf_op jit(solution)/shard_map/all_gather | solution.py:51
  422.2 1.6 fusion.27
  429.7 1.5 constant_dynamic-update-slice_fusion.79
  431.2 1.5 constant_dynamic-update-slice_fusion.78
  433.3 4.2 collective-permute-start.39
  438.8 3.6 collective-permute-done.37
  445.1 42.5 %psum.45 = f32[2,128]{1,0:T(2,128)} all-reduce(f32[2,128]{1,0:T(2,128)} %pad_maximum_fusion.3), channel_id=1, replica_groups=mesh['gx'=2,'gy'=4,'gz'=4] {'gx','gy','gz'}, use_global_device_ids=true, to_apply=%region_9.10 | all-reduce | flops 256 | bytes 2048 | tf_op jit(solution)/shard_map/psum | solution.py:109
  491.8 39.6 %psum.46 = f32[42,128]{1,0:T(8,128)S(1)} all-reduce(f32[42,128]{1,0:T(8,128)S(1)} %pad_maximum_fusion.1), channel_id=1, replica_groups=mesh['gx'=2,'gy'=4,'gz'=4] {'gx','gy','gz'}, use_global_device_ids=true, to_apply=%region_12.13 | all-reduce | flops 5376 | bytes 43008 | tf_op jit(solution)/shard_map/psum | solution.py:103
  532.1 2.8 broadcast_multiply_fusion
  534.9 3.7 convolution_multiply_fusion
  538.9 4.1 collective-permute-done.42
  546.3 3.6 collective-permute-done.43
  550.9 38.9 %all-gather.4 = f32[32,6,128]{2,1,0:T(8,128)S(1)} all-gather(f32[1,6,128]{2,1,0:T(8,128)S(1)} %convolution_bitcast_fusion.11), channel_id=1, replica_groups=mesh['gx'=2,'gy'=4,'gz'=4] {'gx','gy','gz'}, dimensions={0}, use_global_device_ids=true | all-gather | bytes 101376 | tf_op jit(solution)/shard_map/all_gather | solution.py:51
  590.0 1.6 fusion.24
  592.9 1.5 constant_dynamic-update-slice_fusion.94
  595.9 1.5 constant_dynamic-update-slice_fusion.92
  597.4 1.5 constant_dynamic-update-slice_fusion.91
  598.9 1.5 constant_dynamic-update-slice_fusion.90
  601.0 4.2 collective-permute-start.51
  606.7 3.4 collective-permute-done.49
  611.6 42.5 %psum.47 = f32[2,128]{1,0:T(2,128)S(1)} all-reduce(f32[2,128]{1,0:T(2,128)S(1)} %pad_maximum_fusion.4), channel_id=1, replica_groups=mesh['gx'=2,'gy'=4,'gz'=4] {'gx','gy','gz'}, use_global_device_ids=true, to_apply=%region_15.16 | all-reduce | flops 256 | bytes 2048 | tf_op jit(solution)/shard_map/psum | solution.py:109
  654.2 2.1 add_bitcast_fusion
  663.7 2.0 multiply_subtract_fusion
  (424 shorter events, 72.4 us)
Async XLA Ops:
  0.6 46.7 %copy-start = (f32[1,1,1,768,768]{4,3,2,1,0:T(8,128)S(1)}, f32[1,1,1,768,768]{4,3,2,1,0:T(8,128)}, u32[]{:S(2)}) copy-start(f32[1,1,1,768,768]{4,3,2,1,0:T(8,128)} %param.13) | copy-start | bytes 7077892
  40.8 96.2 %copy-start.12 = (f32[6,6,128]{2,1,0:T(8,128)}, f32[6,6,128]{2,1,0:T(8,128)S(1)}, u32[]{:S(2)}) copy-start(f32[6,6,128]{2,1,0:T(8,128)S(1)} %fusion.16) | copy-start | bytes 55300
  41.6 21.3 %collective-permute-start = (f32[1,128,128]{2,1,0:T(8,128)S(1)}, f32[1,128,128]{2,1,0:T(8,128)}, u32[]{:S(2)}, u32[]{:S(2)}) collective-permute-start(f32[1,128,128]{2,1,0:T(8,128)S(1)} %slice.456), channel_id=1, source_target_pairs={{0,16},{16,0},{1,17},{17,1},{2,18},{18,2},{3,19},{19,3},{4,20},{20... | collective-permute-start | bytes 196616 | tf_op jit(solution)/shard_map/ppermute | solution.py:19
  63.7 11.7 %collective-permute-start.1 = (f32[1,128,128]{2,1,0:T(8,128)S(1)}, f32[1,128,128]{2,1,0:T(8,128)}, u32[]{:S(2)}, u32[]{:S(2)}) collective-permute-start(f32[1,128,128]{2,1,0:T(8,128)S(1)} %get-tuple-element.63), channel_id=1, source_target_pairs={{16,0},{0,16},{17,1},{1,17},{18,2},{2,18},{19,3},{3,19},{20,4},{4,... | collective-permute-start | bytes 196616 | tf_op jit(solution)/shard_map/ppermute | solution.py:20
  70.7 7.4 %collective-permute-start.5 = (f32[1,128,128]{2,1,0:T(8,128)S(1)}, f32[1,128,128]{2,1,0:T(8,128)S(1)}, u32[]{:S(2)}, u32[]{:S(2)}) collective-permute-start(f32[1,128,128]{2,1,0:T(8,128)S(1)} %get-tuple-element.58), channel_id=1, source_target_pairs={{1,0},{2,1},{3,2},{0,3},{5,4},{6,5},{7,6},{4,7},{9,8},{10,9},{11,1... | collective-permute-start | bytes 196616 | tf_op jit(solution)/shard_map/ppermute | solution.py:20
  70.7 7.3 %collective-permute-start.4 = (f32[1,128,128]{2,1,0:T(8,128)S(1)}, f32[1,128,128]{2,1,0:T(8,128)S(1)}, u32[]{:S(2)}, u32[]{:S(2)}) collective-permute-start(f32[1,128,128]{2,1,0:T(8,128)S(1)} %get-tuple-element.60), channel_id=1, source_target_pairs={{0,1},{1,2},{2,3},{3,0},{4,5},{5,6},{6,7},{7,4},{8,9},{9,10},{10,1... | collective-permute-start | bytes 196616 | tf_op jit(solution)/shard_map/ppermute | solution.py:19
  71.2 6.8 %collective-permute-start.2 = (f32[1,128,128]{2,1,0:T(8,128)S(1)}, f32[1,128,128]{2,1,0:T(8,128)S(1)}, u32[]{:S(2)}, u32[]{:S(2)}) collective-permute-start(f32[1,128,128]{2,1,0:T(8,128)S(1)} %get-tuple-element.61), channel_id=1, source_target_pairs={{0,4},{4,8},{8,12},{12,0},{1,5},{5,9},{9,13},{13,1},{2,6},{6,10},{... | collective-permute-start | bytes 196616 | tf_op jit(solution)/shard_map/ppermute | solution.py:19
  71.2 6.8 %collective-permute-start.3 = (f32[1,128,128]{2,1,0:T(8,128)S(1)}, f32[1,128,128]{2,1,0:T(8,128)S(1)}, u32[]{:S(2)}, u32[]{:S(2)}) collective-permute-start(f32[1,128,128]{2,1,0:T(8,128)S(1)} %get-tuple-element.62), channel_id=1, source_target_pairs={{4,0},{8,4},{12,8},{0,12},{5,1},{9,5},{13,9},{1,13},{6,2},{10,6},{... | collective-permute-start | bytes 196616 | tf_op jit(solution)/shard_map/ppermute | solution.py:20
  78.9 57.9 %copy-start.38 = (f32[1,1,1,6,192]{4,2,3,1,0:T(1,128)S(1)}, f32[1,1,1,6,192]{4,2,3,1,0:T(1,128)}, u32[]{:S(2)}) copy-start(f32[1,1,1,6,192]{4,2,3,1,0:T(1,128)} %param.17) | copy-start | bytes 13828
  82.6 4.3 collective-permute-start.6
  87.0 11.1 %collective-permute-start.11 = (f32[1,128,128]{2,1,0:T(8,128)S(1)}, f32[1,128,128]{2,1,0:T(8,128)S(1)}, u32[]{:S(2)}, u32[]{:S(2)}) collective-permute-start(f32[1,128,128]{2,1,0:T(8,128)S(1)} %get-tuple-element.52), channel_id=1, source_target_pairs={{1,0},{2,1},{3,2},{0,3},{5,4},{6,5},{7,6},{4,7},{9,8},{10,9},{11,1... | collective-permute-start | bytes 196616 | tf_op jit(solution)/shard_map/ppermute | solution.py:20
  87.0 11.0 %collective-permute-start.10 = (f32[1,128,128]{2,1,0:T(8,128)S(1)}, f32[1,128,128]{2,1,0:T(8,128)S(1)}, u32[]{:S(2)}, u32[]{:S(2)}) collective-permute-start(f32[1,128,128]{2,1,0:T(8,128)S(1)} %get-tuple-element.54), channel_id=1, source_target_pairs={{0,1},{1,2},{2,3},{3,0},{4,5},{5,6},{6,7},{7,4},{8,9},{9,10},{10,1... | collective-permute-start | bytes 196616 | tf_op jit(solution)/shard_map/ppermute | solution.py:19
  87.5 8.9 %collective-permute-start.8 = (f32[1,128,128]{2,1,0:T(8,128)S(1)}, f32[1,128,128]{2,1,0:T(8,128)S(1)}, u32[]{:S(2)}, u32[]{:S(2)}) collective-permute-start(f32[1,128,128]{2,1,0:T(8,128)S(1)} %get-tuple-element.55), channel_id=1, source_target_pairs={{0,4},{4,8},{8,12},{12,0},{1,5},{5,9},{9,13},{13,1},{2,6},{6,10},{... | collective-permute-start | bytes 196616 | tf_op jit(solution)/shard_map/ppermute | solution.py:19
  92.1 5.9 collective-permute-start.9
  92.1 4.3 collective-permute-start.7
  137.8 58.8 %copy-start.90 = (f32[40]{0:T(128)S(1)}, f32[40]{0:T(128)}, u32[]{:S(2)}) copy-start(f32[40]{0:T(128)} %param.20) | copy-start | bytes 484
  137.8 4.4 collective-permute-start.12
  142.2 9.3 %collective-permute-start.17 = (f32[1,128,128]{2,1,0:T(8,128)S(1)}, f32[1,128,128]{2,1,0:T(8,128)S(1)}, u32[]{:S(2)}, u32[]{:S(2)}) collective-permute-start(f32[1,128,128]{2,1,0:T(8,128)S(1)} %get-tuple-element.46), channel_id=1, source_target_pairs={{1,0},{2,1},{3,2},{0,3},{5,4},{6,5},{7,6},{4,7},{9,8},{10,9},{11,1... | collective-permute-start | bytes 196616 | tf_op jit(solution)/shard_map/ppermute | solution.py:20
  142.3 9.2 %collective-permute-start.16 = (f32[1,128,128]{2,1,0:T(8,128)S(1)}, f32[1,128,128]{2,1,0:T(8,128)S(1)}, u32[]{:S(2)}, u32[]{:S(2)}) collective-permute-start(f32[1,128,128]{2,1,0:T(8,128)S(1)} %get-tuple-element.48), channel_id=1, source_target_pairs={{0,1},{1,2},{2,3},{3,0},{4,5},{5,6},{6,7},{7,4},{8,9},{9,10},{10,1... | collective-permute-start | bytes 196616 | tf_op jit(solution)/shard_map/ppermute | solution.py:19
  142.8 8.6 %collective-permute-start.14 = (f32[1,128,128]{2,1,0:T(8,128)S(1)}, f32[1,128,128]{2,1,0:T(8,128)S(1)}, u32[]{:S(2)}, u32[]{:S(2)}) collective-permute-start(f32[1,128,128]{2,1,0:T(8,128)S(1)} %get-tuple-element.49), channel_id=1, source_target_pairs={{0,4},{4,8},{8,12},{12,0},{1,5},{5,9},{9,13},{13,1},{2,6},{6,10},{... | collective-permute-start | bytes 196616 | tf_op jit(solution)/shard_map/ppermute | solution.py:19
  142.8 8.7 %collective-permute-start.15 = (f32[1,128,128]{2,1,0:T(8,128)S(1)}, f32[1,128,128]{2,1,0:T(8,128)S(1)}, u32[]{:S(2)}, u32[]{:S(2)}) collective-permute-start(f32[1,128,128]{2,1,0:T(8,128)S(1)} %get-tuple-element.50), channel_id=1, source_target_pairs={{4,0},{8,4},{12,8},{0,12},{5,1},{9,5},{13,9},{1,13},{6,2},{10,6},{... | collective-permute-start | bytes 196616 | tf_op jit(solution)/shard_map/ppermute | solution.py:20
  146.9 4.4 collective-permute-start.13
  202.2 4.3 collective-permute-start.18
  206.5 7.0 %collective-permute-start.23 = (f32[1,128,128]{2,1,0:T(8,128)S(1)}, f32[1,128,128]{2,1,0:T(8,128)S(1)}, u32[]{:S(2)}, u32[]{:S(2)}) collective-permute-start(f32[1,128,128]{2,1,0:T(8,128)S(1)} %get-tuple-element.40), channel_id=1, source_target_pairs={{1,0},{2,1},{3,2},{0,3},{5,4},{6,5},{7,6},{4,7},{9,8},{10,9},{11,1... | collective-permute-start | bytes 196616 | tf_op jit(solution)/shard_map/ppermute | solution.py:20
  206.6 6.9 %collective-permute-start.22 = (f32[1,128,128]{2,1,0:T(8,128)S(1)}, f32[1,128,128]{2,1,0:T(8,128)S(1)}, u32[]{:S(2)}, u32[]{:S(2)}) collective-permute-start(f32[1,128,128]{2,1,0:T(8,128)S(1)} %get-tuple-element.42), channel_id=1, source_target_pairs={{0,1},{1,2},{2,3},{3,0},{4,5},{5,6},{6,7},{7,4},{8,9},{9,10},{10,1... | collective-permute-start | bytes 196616 | tf_op jit(solution)/shard_map/ppermute | solution.py:19
  207.1 6.3 collective-permute-start.20
  208.1 5.3 collective-permute-start.21
  209.1 4.3 collective-permute-start.19
  257.8 8.7 %collective-permute-start.24 = (f32[1,128,128]{2,1,0:T(8,128)S(1)}, f32[1,128,128]{2,1,0:T(8,128)S(1)}, u32[]{:S(2)}, u32[]{:S(2)}) collective-permute-start(f32[1,128,128]{2,1,0:T(8,128)S(1)} %slice.480), channel_id=1, source_target_pairs={{0,16},{16,0},{1,17},{17,1},{2,18},{18,2},{3,19},{19,3},{4,20},{20... | collective-permute-start | bytes 196616 | tf_op jit(solution)/shard_map/ppermute | solution.py:19
  266.6 9.8 %collective-permute-start.29 = (f32[1,128,128]{2,1,0:T(8,128)S(1)}, f32[1,128,128]{2,1,0:T(8,128)S(1)}, u32[]{:S(2)}, u32[]{:S(2)}) collective-permute-start(f32[1,128,128]{2,1,0:T(8,128)S(1)} %get-tuple-element.34), channel_id=1, source_target_pairs={{1,0},{2,1},{3,2},{0,3},{5,4},{6,5},{7,6},{4,7},{9,8},{10,9},{11,1... | collective-permute-start | bytes 196616 | tf_op jit(solution)/shard_map/ppermute | solution.py:20
  266.7 9.7 %collective-permute-start.28 = (f32[1,128,128]{2,1,0:T(8,128)S(1)}, f32[1,128,128]{2,1,0:T(8,128)S(1)}, u32[]{:S(2)}, u32[]{:S(2)}) collective-permute-start(f32[1,128,128]{2,1,0:T(8,128)S(1)} %get-tuple-element.36), channel_id=1, source_target_pairs={{0,1},{1,2},{2,3},{3,0},{4,5},{5,6},{6,7},{7,4},{8,9},{9,10},{10,1... | collective-permute-start | bytes 196616 | tf_op jit(solution)/shard_map/ppermute | solution.py:19
  267.1 9.1 %collective-permute-start.26 = (f32[1,128,128]{2,1,0:T(8,128)S(1)}, f32[1,128,128]{2,1,0:T(8,128)S(1)}, u32[]{:S(2)}, u32[]{:S(2)}) collective-permute-start(f32[1,128,128]{2,1,0:T(8,128)S(1)} %get-tuple-element.37), channel_id=1, source_target_pairs={{0,4},{4,8},{8,12},{12,0},{1,5},{5,9},{9,13},{13,1},{2,6},{6,10},{... | collective-permute-start | bytes 196616 | tf_op jit(solution)/shard_map/ppermute | solution.py:19
  267.2 9.1 %collective-permute-start.27 = (f32[1,128,128]{2,1,0:T(8,128)S(1)}, f32[1,128,128]{2,1,0:T(8,128)S(1)}, u32[]{:S(2)}, u32[]{:S(2)}) collective-permute-start(f32[1,128,128]{2,1,0:T(8,128)S(1)} %get-tuple-element.38), channel_id=1, source_target_pairs={{4,0},{8,4},{12,8},{0,12},{5,1},{9,5},{13,9},{1,13},{6,2},{10,6},{... | collective-permute-start | bytes 196616 | tf_op jit(solution)/shard_map/ppermute | solution.py:20
  271.3 4.9 collective-permute-start.25
  370.8 4.3 collective-permute-start.30
  375.2 7.3 %collective-permute-start.35 = (f32[1,128,128]{2,1,0:T(8,128)S(1)}, f32[1,128,128]{2,1,0:T(8,128)S(1)}, u32[]{:S(2)}, u32[]{:S(2)}) collective-permute-start(f32[1,128,128]{2,1,0:T(8,128)S(1)} %get-tuple-element.28), channel_id=1, source_target_pairs={{1,0},{2,1},{3,2},{0,3},{5,4},{6,5},{7,6},{4,7},{9,8},{10,9},{11,1... | collective-permute-start | bytes 196616 | tf_op jit(solution)/shard_map/ppermute | solution.py:20
  375.2 7.2 %collective-permute-start.34 = (f32[1,128,128]{2,1,0:T(8,128)S(1)}, f32[1,128,128]{2,1,0:T(8,128)S(1)}, u32[]{:S(2)}, u32[]{:S(2)}) collective-permute-start(f32[1,128,128]{2,1,0:T(8,128)S(1)} %get-tuple-element.30), channel_id=1, source_target_pairs={{0,1},{1,2},{2,3},{3,0},{4,5},{5,6},{6,7},{7,4},{8,9},{9,10},{10,1... | collective-permute-start | bytes 196616 | tf_op jit(solution)/shard_map/ppermute | solution.py:19
  375.7 6.6 collective-permute-start.32
  376.7 5.7 collective-permute-start.33
  377.8 4.5 collective-permute-start.31
  422.0 21.7 %copy-start.20 = (f32[6,128,128]{2,1,0:T(8,128)S(1)}, f32[6,128,128]{2,1,0:T(8,128)}, u32[]{:S(2)}) copy-start(f32[6,128,128]{2,1,0:T(8,128)} %copy-done.19) | copy-start | bytes 1179652
  422.2 21.6 %copy-start.9 = (f32[6,128,128]{2,1,0:T(8,128)S(1)}, f32[6,128,128]{2,1,0:T(8,128)}, u32[]{:S(2)}) copy-start(f32[6,128,128]{2,1,0:T(8,128)} %get-tuple-element.69) | copy-start | bytes 1179652
  423.8 8.9 %collective-permute-start.36 = (f32[1,128,128]{2,1,0:T(8,128)S(1)}, f32[1,128,128]{2,1,0:T(8,128)S(1)}, u32[]{:S(2)}, u32[]{:S(2)}) collective-permute-start(f32[1,128,128]{2,1,0:T(8,128)S(1)} %slice.494), channel_id=1, source_target_pairs={{0,16},{16,0},{1,17},{17,1},{2,18},{18,2},{3,19},{19,3},{4,20},{20... | collective-permute-start | bytes 196616 | tf_op jit(solution)/shard_map/ppermute | solution.py:19
  432.7 9.8 %collective-permute-start.41 = (f32[1,128,128]{2,1,0:T(8,128)S(1)}, f32[1,128,128]{2,1,0:T(8,128)S(1)}, u32[]{:S(2)}, u32[]{:S(2)}) collective-permute-start(f32[1,128,128]{2,1,0:T(8,128)S(1)} %get-tuple-element.22), channel_id=1, source_target_pairs={{1,0},{2,1},{3,2},{0,3},{5,4},{6,5},{7,6},{4,7},{9,8},{10,9},{11,1... | collective-permute-start | bytes 196616 | tf_op jit(solution)/shard_map/ppermute | solution.py:20
  432.8 9.7 %collective-permute-start.40 = (f32[1,128,128]{2,1,0:T(8,128)S(1)}, f32[1,128,128]{2,1,0:T(8,128)S(1)}, u32[]{:S(2)}, u32[]{:S(2)}) collective-permute-start(f32[1,128,128]{2,1,0:T(8,128)S(1)} %get-tuple-element.24), channel_id=1, source_target_pairs={{0,1},{1,2},{2,3},{3,0},{4,5},{5,6},{6,7},{7,4},{8,9},{9,10},{10,1... | collective-permute-start | bytes 196616 | tf_op jit(solution)/shard_map/ppermute | solution.py:19
  433.3 9.1 %collective-permute-start.38 = (f32[1,128,128]{2,1,0:T(8,128)S(1)}, f32[1,128,128]{2,1,0:T(8,128)S(1)}, u32[]{:S(2)}, u32[]{:S(2)}) collective-permute-start(f32[1,128,128]{2,1,0:T(8,128)S(1)} %get-tuple-element.25), channel_id=1, source_target_pairs={{0,4},{4,8},{8,12},{12,0},{1,5},{5,9},{9,13},{13,1},{2,6},{6,10},{... | collective-permute-start | bytes 196616 | tf_op jit(solution)/shard_map/ppermute | solution.py:19
  433.3 9.1 %collective-permute-start.39 = (f32[1,128,128]{2,1,0:T(8,128)S(1)}, f32[1,128,128]{2,1,0:T(8,128)S(1)}, u32[]{:S(2)}, u32[]{:S(2)}) collective-permute-start(f32[1,128,128]{2,1,0:T(8,128)S(1)} %get-tuple-element.26), channel_id=1, source_target_pairs={{4,0},{8,4},{12,8},{0,12},{5,1},{9,5},{13,9},{1,13},{6,2},{10,6},{... | collective-permute-start | bytes 196616 | tf_op jit(solution)/shard_map/ppermute | solution.py:20
  437.4 4.9 collective-permute-start.37
  538.7 4.3 collective-permute-start.42
  543.0 7.1 %collective-permute-start.47 = (f32[1,128,128]{2,1,0:T(8,128)S(1)}, f32[1,128,128]{2,1,0:T(8,128)S(1)}, u32[]{:S(2)}, u32[]{:S(2)}) collective-permute-start(f32[1,128,128]{2,1,0:T(8,128)S(1)} %get-tuple-element.16), channel_id=1, source_target_pairs={{1,0},{2,1},{3,2},{0,3},{5,4},{6,5},{7,6},{4,7},{9,8},{10,9},{11,1... | collective-permute-start | bytes 196616 | tf_op jit(solution)/shard_map/ppermute | solution.py:20
  543.1 7.0 %collective-permute-start.46 = (f32[1,128,128]{2,1,0:T(8,128)S(1)}, f32[1,128,128]{2,1,0:T(8,128)S(1)}, u32[]{:S(2)}, u32[]{:S(2)}) collective-permute-start(f32[1,128,128]{2,1,0:T(8,128)S(1)} %get-tuple-element.18), channel_id=1, source_target_pairs={{0,1},{1,2},{2,3},{3,0},{4,5},{5,6},{6,7},{7,4},{8,9},{9,10},{10,1... | collective-permute-start | bytes 196616 | tf_op jit(solution)/shard_map/ppermute | solution.py:19
  543.6 6.4 collective-permute-start.44
  544.6 5.4 collective-permute-start.45
  545.7 4.3 collective-permute-start.43
  589.9 21.6 %copy-start.22 = (f32[6,128,128]{2,1,0:T(8,128)S(1)}, f32[6,128,128]{2,1,0:T(8,128)}, u32[]{:S(2)}) copy-start(f32[6,128,128]{2,1,0:T(8,128)} %copy-done.21) | copy-start | bytes 1179652
  591.7 62.4 %copy-start.10 = (f32[6,128,128]{2,1,0:T(8,128)S(1)}, f32[6,128,128]{2,1,0:T(8,128)}, u32[]{:S(2)}) copy-start(f32[6,128,128]{2,1,0:T(8,128)} %get-tuple-element.69) | copy-start | bytes 1179652
  591.7 62.4 %copy-start.92 = (f32[128]{0:T(128)S(1)}, f32[128]{0:T(128)}, u32[]{:S(2)}) copy-start(f32[128]{0:T(128)} %copy-done.91) | copy-start | bytes 1540
  591.7 62.4 %copy-start.94 = (f32[128]{0:T(128)S(1)}, f32[128]{0:T(128)}, u32[]{:S(2)}) copy-start(f32[128]{0:T(128)} %copy-done.93) | copy-start | bytes 1540
  591.7 8.7 %collective-permute-start.48 = (f32[1,128,128]{2,1,0:T(8,128)S(1)}, f32[1,128,128]{2,1,0:T(8,128)S(1)}, u32[]{:S(2)}, u32[]{:S(2)}) collective-permute-start(f32[1,128,128]{2,1,0:T(8,128)S(1)} %slice.509), channel_id=1, source_target_pairs={{0,16},{16,0},{1,17},{17,1},{2,18},{18,2},{3,19},{19,3},{4,20},{20... | collective-permute-start | bytes 196616 | tf_op jit(solution)/shard_map/ppermute | solution.py:19
  600.4 9.8 %collective-permute-start.53 = (f32[1,128,128]{2,1,0:T(8,128)S(1)}, f32[1,128,128]{2,1,0:T(8,128)S(1)}, u32[]{:S(2)}, u32[]{:S(2)}) collective-permute-start(f32[1,128,128]{2,1,0:T(8,128)S(1)} %get-tuple-element.10), channel_id=1, source_target_pairs={{1,0},{2,1},{3,2},{0,3},{5,4},{6,5},{7,6},{4,7},{9,8},{10,9},{11,1... | collective-permute-start | bytes 196616 | tf_op jit(solution)/shard_map/ppermute | solution.py:20
  600.5 9.7 %collective-permute-start.52 = (f32[1,128,128]{2,1,0:T(8,128)S(1)}, f32[1,128,128]{2,1,0:T(8,128)S(1)}, u32[]{:S(2)}, u32[]{:S(2)}) collective-permute-start(f32[1,128,128]{2,1,0:T(8,128)S(1)} %get-tuple-element.12), channel_id=1, source_target_pairs={{0,1},{1,2},{2,3},{3,0},{4,5},{5,6},{6,7},{7,4},{8,9},{9,10},{10,1... | collective-permute-start | bytes 196616 | tf_op jit(solution)/shard_map/ppermute | solution.py:19
  601.0 9.1 %collective-permute-start.50 = (f32[1,128,128]{2,1,0:T(8,128)S(1)}, f32[1,128,128]{2,1,0:T(8,128)S(1)}, u32[]{:S(2)}, u32[]{:S(2)}) collective-permute-start(f32[1,128,128]{2,1,0:T(8,128)S(1)} %get-tuple-element.13), channel_id=1, source_target_pairs={{0,4},{4,8},{8,12},{12,0},{1,5},{5,9},{9,13},{13,1},{2,6},{6,10},{... | collective-permute-start | bytes 196616 | tf_op jit(solution)/shard_map/ppermute | solution.py:19
  601.0 9.1 %collective-permute-start.51 = (f32[1,128,128]{2,1,0:T(8,128)S(1)}, f32[1,128,128]{2,1,0:T(8,128)S(1)}, u32[]{:S(2)}, u32[]{:S(2)}) collective-permute-start(f32[1,128,128]{2,1,0:T(8,128)S(1)} %get-tuple-element.14), channel_id=1, source_target_pairs={{4,0},{8,4},{12,8},{0,12},{5,1},{9,5},{13,9},{1,13},{6,2},{10,6},{... | collective-permute-start | bytes 196616 | tf_op jit(solution)/shard_map/ppermute | solution.py:20
  605.2 4.9 collective-permute-start.49
  (86 other events, 424.6 us)
where the time goes:
time: 668 us; the launch traced here: 666 us
  blocking collectives  442 us (66%)
  other arithmetic  60.4 us (9%)
  starting transfers between devices  49.7 us (7%)
  waiting for transfers between devices  45.8 us (7%)
  matrix products  34.5 us (5%)
  local copies, waits for them, and re-layouts  29.8 us (4%)
    all_gather x5, blocking collectives, coarse_solve(): lax.all_gather(loads, ('gx', 'gy', 'gz'), axis=0, tiled=True)  192 us
    psum x3, blocking collectives, per_device(): lax.psum(jnp.stack([plus_inner(direction, image_now), plus_inner(directio...  127 us
    psum x3, blocking collectives, per_device(): totals = lax.psum(local_rows, ('gx', 'gy', 'gz'))  122 us
    unnamed x76, other arithmetic  32.8 us
    ppermute x27, starting transfers between devices, extended(): after = lax.ppermute(initial, axis, down)  29.9 us
    ppermute x27, waiting for transfers between devices, extended(): after = lax.ppermute(initial, axis, down)  28.2 us
    ppermute x27, starting transfers between devices, extended(): before = lax.ppermute(last, axis, up)  19.8 us
    ppermute x27, waiting for transfers between devices, extended(): before = lax.ppermute(last, axis, up)  17.5 us
  transfers between devices with their start and end apart: 54, of which 15 were waited for; matrix products, arithmetic and copies ran while one was open for 9% of the time, Pallas kernels for 0%

commit v1 on v0

--- a/solution.py
+++ b/solution.py
@@ -2,6 +2,7 @@
 import jax.numpy as jnp
 from jax import lax
 from jax.sharding import PartitionSpec as P
+from jax.lax import psum
 
 STORED = 40
 ITERS = 3
@@ -100,7 +101,7 @@
         if images:
             own_rows = jnp.stack([plus_inner(images[index], resid) for index in range(len(images))])
             local_rows = jnp.concatenate([local_rows, own_rows], axis=0)
-        totals = lax.psum(local_rows, ("gx", "gy", "gz"))
+        totals = psum(psum(local_rows, axis_name=("gy", "gz")), axis_name="gx")
         beta = totals[:STORED] / stored_curv[:, None]
         direction = resid - jnp.einsum("isf,ir->sfr", dirs_store, beta, precision=precise)
         for index in range(len(directions)):

time: 668 us -> 740 us (1.11)
  blocking collectives: 442 us -> 494 us
  starting transfers between devices: 49.7 us -> 77.5 us
  waiting for transfers between devices: 45.8 us -> 34.4 us
    psum x3 -> x6, blocking collectives: 122 us -> 177 us  [per_device(): totals = psum(psum(local_rows, axis_name=('gy', 'gz')), axis_name='gx')]
    ppermute x27, starting transfers between devices: 29.9 us -> 60.6 us  [extended(): after = lax.ppermute(initial, axis, down)]
  transfers between devices with their start and end apart: 54 -> 54, of which waited for: 15 -> 14; matrix products, arithmetic and copies ran while one was open for 9% -> 8% of each run, Pallas kernels for 0% -> 0%
where the time goes in v1:
time: 740 us; the launch traced here: 738 us
  blocking collectives  494 us (67%)
  starting transfers between devices  77.5 us (10%)
  other arithmetic  64.4 us (9%)
  matrix products  34.5 us (5%)
  waiting for transfers between devices  34.4 us (5%)
  local copies, waits for them, and re-layouts  29.9 us (4%)
    all_gather x5, blocking collectives, coarse_solve(): lax.all_gather(loads, ('gx', 'gy', 'gz'), axis=0, tiled=True)  187 us
    psum x6, blocking collectives, per_device(): totals = psum(psum(local_rows, axis_name=('gy', 'gz')), axis_name='gx')  177 us
    psum x3, blocking collectives, per_device(): lax.psum(jnp.stack([plus_inner(direction, image_now), plus_inner(directio...  130 us
    ppermute x27, starting transfers between devices, extended(): after = lax.ppermute(initial, axis, down)  60.6 us
    unnamed x76, other arithmetic  36.1 us
    ppermute x27, waiting for transfers between devices, extended(): after = lax.ppermute(initial, axis, down)  22.5 us
    ppermute x27, starting transfers between devices, extended(): before = lax.ppermute(last, axis, up)  17 us
    dot_general x4, matrix products, operate(): return jnp.dot(flex_face, flat, precision=precise).reshape(layout)  14.8 us
  transfers between devices with their start and end apart: 54, of which 14 were waited for; matrix products, arithmetic and copies ran while one was open for 8% of the time, Pallas kernels for 0%

profile of v1, /device:TPU:10, one launch (start us, length us, event | category | flops | bytes accessed | tf_op | source)
XLA Modules:
  0.0 737.6 jit_solution(11555076397813237771)
XLA Ops:
  1.5 37.6 %all-gather = f32[1,1,1,192,128]{4,2,1,0,3:T(1,128)S(1)} all-gather(f32[1,1,1,6,128]{4,2,1,0,3:T(1,128)} %bitcast.275), channel_id=2, replica_groups=mesh['gx'=2,'gy'=4,'gz'=4] {'gx','gy','gz'}, dimensions={3}, use_global_device_ids=true | all-gather | bytes 101376 | tf_op jit(solution)/shard_map/all_gather | solution.py:52
  41.6 1.6 collective-permute-start
  43.9 3.4 scatter_custom_fusion
  47.3 3.5 gather_fusion
  50.8 3.3 broadcast_select_fusion
  54.1 3.0 copy.40
  57.1 5.7 gather_fusion.1
  64.3 3.3 select_bitcast_fusion
  67.6 3.1 copy.41
  71.2 4.2 collective-permute-start.3
  76.2 1.8 collective-permute-done.2
  78.8 3.7 fusion.4
  82.5 1.6 collective-permute-start.6
  84.1 2.8 collective-permute-done.6
  87.5 4.6 collective-permute-start.8
  94.2 2.2 collective-permute-done.7
  96.4 1.6 collective-permute-done.9
  99.1 37.6 %all-gather.1 = f32[32,6,128]{2,1,0:T(8,128)S(1)} all-gather(f32[1,6,128]{2,1,0:T(8,128)S(1)} %convolution_bitcast_fusion.14), channel_id=1, replica_groups=mesh['gx'=2,'gy'=4,'gz'=4] {'gx','gy','gz'}, dimensions={0}, use_global_device_ids=true | all-gather | bytes 101376 | tf_op jit(solution)/shard_map/all_gather | solution.py:52
  142.7 4.2 collective-permute-start.15
  148.4 3.0 collective-permute-done.13
  153.0 54.6 %psum.63 = f32[40,128]{1,0:T(8,128)S(1)} all-reduce(f32[40,128]{1,0:T(8,128)S(1)} %convolution_bitcast_fusion.5), channel_id=1, replica_groups=mesh['gx'=2,'gy'=4,'gz'=4] {'gy','gz'}, use_global_device_ids=true, to_apply=%region_1.2 | all-reduce | flops 5120 | bytes 40960 | tf_op jit(solution)/shard_map/psum | solution.py:104
  207.6 7.6 %psum.64 = f32[40,128]{1,0:T(8,128)} all-reduce(f32[40,128]{1,0:T(8,128)S(1)} %psum.63), channel_id=1, replica_groups=mesh['gx'=2,'gy'=4,'gz'=4] {'gx'}, use_global_device_ids=true, to_apply=%region_2.3 | all-reduce | flops 5120 | bytes 40960 | tf_op jit(solution)/shard_map/psum | solution.py:104
  215.2 1.8 broadcast_multiply_fusion.2
  217.0 3.7 convolution_multiply_fusion.2
  220.8 1.8 collective-permute-start.18
  227.2 8.4 %collective-permute-start.21 = (f32[1,128,128]{2,1,0:T(8,128)S(1)}, f32[1,128,128]{2,1,0:T(8,128)S(1)}, u32[]{:S(2)}, u32[]{:S(2)}) collective-permute-start(f32[1,128,128]{2,1,0:T(8,128)S(1)} %get-tuple-element.44), channel_id=1, source_target_pairs={{4,0},{8,4},{12,8},{0,12},{5,1},{9,5},{13,9},{1,13},{6,2},{10,6},{... | collective-permute-start | bytes 196616 | tf_op jit(solution)/shard_map/ppermute | solution.py:21
  236.5 3.4 collective-permute-done.19
  240.7 39.0 %all-gather.2 = f32[32,6,128]{2,1,0:T(8,128)} all-gather(f32[1,6,128]{2,1,0:T(8,128)S(1)} %convolution_bitcast_fusion.13), channel_id=1, replica_groups=mesh['gx'=2,'gy'=4,'gz'=4] {'gx','gy','gz'}, dimensions={0}, use_global_device_ids=true | all-gather | bytes 101376 | tf_op jit(solution)/shard_map/all_gather | solution.py:52
  279.7 1.6 reshape.910
  282.3 1.6 fusion.30
  291.7 1.8 collective-permute-start.29
  293.5 4.2 collective-permute-start.27
  297.7 1.7 collective-permute-start.25
  300.0 2.0 collective-permute-done.25
  304.2 43.4 %psum.65 = f32[2,128]{1,0:T(2,128)S(1)} all-reduce(f32[2,128]{1,0:T(2,128)S(1)} %pad_maximum_fusion.2), channel_id=1, replica_groups=mesh['gx'=2,'gy'=4,'gz'=4] {'gx','gy','gz'}, use_global_device_ids=true, to_apply=%region_5.6 | all-reduce | flops 256 | bytes 2048 | tf_op jit(solution)/shard_map/psum | solution.py:110
  351.4 49.3 %psum.66 = f32[41,128]{1,0:T(8,128)S(1)} all-reduce(f32[41,128]{1,0:T(8,128)S(1)} %pad_maximum_fusion), channel_id=1, replica_groups=mesh['gx'=2,'gy'=4,'gz'=4] {'gy','gz'}, use_global_device_ids=true, to_apply=%region_7.8 | all-reduce | flops 5248 | bytes 41984 | tf_op jit(solution)/shard_map/psum | solution.py:104
  400.7 8.0 %psum.67 = f32[41,128]{1,0:T(8,128)S(1)} all-reduce(f32[41,128]{1,0:T(8,128)S(1)} %psum.66), channel_id=1, replica_groups=mesh['gx'=2,'gy'=4,'gz'=4] {'gx'}, use_global_device_ids=true, to_apply=%region_8.9 | all-reduce | flops 5248 | bytes 41984 | tf_op jit(solution)/shard_map/psum | solution.py:104
  409.3 2.6 broadcast_multiply_fusion.1
  411.9 3.7 convolution_multiply_fusion.1
  416.7 3.3 collective-permute-done.30
  420.6 8.4 %collective-permute-start.33 = (f32[1,128,128]{2,1,0:T(8,128)S(1)}, f32[1,128,128]{2,1,0:T(8,128)S(1)}, u32[]{:S(2)}, u32[]{:S(2)}) collective-permute-start(f32[1,128,128]{2,1,0:T(8,128)S(1)} %get-tuple-element.32), channel_id=1, source_target_pairs={{4,0},{8,4},{12,8},{0,12},{5,1},{9,5},{13,9},{1,13},{6,2},{10,6},{... | collective-permute-start | bytes 196616 | tf_op jit(solution)/shard_map/ppermute | solution.py:21
  430.5 2.8 collective-permute-done.31
  434.2 36.5 %all-gather.3 = f32[32,6,128]{2,1,0:T(8,128)S(1)} all-gather(f32[1,6,128]{2,1,0:T(8,128)S(1)} %convolution_bitcast_fusion.12), channel_id=1, replica_groups=mesh['gx'=2,'gy'=4,'gz'=4] {'gx','gy','gz'}, dimensions={0}, use_global_device_ids=true | all-gather | bytes 101376 | tf_op jit(solution)/shard_map/all_gather | solution.py:52
  471.0 1.6 fusion.27
  481.0 1.7 collective-permute-start.41
  482.7 4.2 collective-permute-start.39
  488.7 2.4 collective-permute-done.37
  493.9 43.3 %psum.68 = f32[2,128]{1,0:T(2,128)} all-reduce(f32[2,128]{1,0:T(2,128)} %pad_maximum_fusion.3), channel_id=1, replica_groups=mesh['gx'=2,'gy'=4,'gz'=4] {'gx','gy','gz'}, use_global_device_ids=true, to_apply=%region_11.12 | all-reduce | flops 256 | bytes 2048 | tf_op jit(solution)/shard_map/psum | solution.py:110
  541.4 49.4 %psum.69 = f32[42,128]{1,0:T(8,128)S(1)} all-reduce(f32[42,128]{1,0:T(8,128)S(1)} %pad_maximum_fusion.1), channel_id=1, replica_groups=mesh['gx'=2,'gy'=4,'gz'=4] {'gy','gz'}, use_global_device_ids=true, to_apply=%region_14.15 | all-reduce | flops 5376 | bytes 43008 | tf_op jit(solution)/shard_map/psum | solution.py:104
  590.8 8.0 %psum.70 = f32[42,128]{1,0:T(8,128)S(1)} all-reduce(f32[42,128]{1,0:T(8,128)S(1)} %psum.69), channel_id=1, replica_groups=mesh['gx'=2,'gy'=4,'gz'=4] {'gx'}, use_global_device_ids=true, to_apply=%region_15.16 | all-reduce | flops 5376 | bytes 43008 | tf_op jit(solution)/shard_map/psum | solution.py:104
  599.5 2.8 broadcast_multiply_fusion
  602.3 3.7 convolution_multiply_fusion
  607.1 3.3 collective-permute-done.42
  611.0 8.5 %collective-permute-start.45 = (f32[1,128,128]{2,1,0:T(8,128)S(1)}, f32[1,128,128]{2,1,0:T(8,128)S(1)}, u32[]{:S(2)}, u32[]{:S(2)}) collective-permute-start(f32[1,128,128]{2,1,0:T(8,128)S(1)} %get-tuple-element.20), channel_id=1, source_target_pairs={{4,0},{8,4},{12,8},{0,12},{5,1},{9,5},{13,9},{1,13},{6,2},{10,6},{... | collective-permute-start | bytes 196616 | tf_op jit(solution)/shard_map/ppermute | solution.py:21
  620.9 2.8 collective-permute-done.43
  624.7 36.3 %all-gather.4 = f32[32,6,128]{2,1,0:T(8,128)S(1)} all-gather(f32[1,6,128]{2,1,0:T(8,128)S(1)} %convolution_bitcast_fusion.11), channel_id=1, replica_groups=mesh['gx'=2,'gy'=4,'gz'=4] {'gx','gy','gz'}, dimensions={0}, use_global_device_ids=true | all-gather | bytes 101376 | tf_op jit(solution)/shard_map/all_gather | solution.py:52
  661.2 1.6 fusion.24
  668.2 1.5 constant_dynamic-update-slice_fusion.91
  671.3 1.7 collective-permute-start.53
  673.0 4.2 collective-permute-start.51
  679.0 2.4 collective-permute-done.49
  683.0 43.1 %psum.71 = f32[2,128]{1,0:T(2,128)S(1)} all-reduce(f32[2,128]{1,0:T(2,128)S(1)} %pad_maximum_fusion.4), channel_id=1, replica_groups=mesh['gx'=2,'gy'=4,'gz'=4] {'gx','gy','gz'}, use_global_device_ids=true, to_apply=%region_18.19 | all-reduce | flops 256 | bytes 2048 | tf_op jit(solution)/shard_map/psum | solution.py:110
  726.1 2.1 add_bitcast_fusion
  735.6 2.0 multiply_subtract_fusion
  (421 shorter events, 85.3 us)
Async XLA Ops:
  0.6 46.7 %copy-start = (f32[1,1,1,768,768]{4,3,2,1,0:T(8,128)S(1)}, f32[1,1,1,768,768]{4,3,2,1,0:T(8,128)}, u32[]{:S(2)}) copy-start(f32[1,1,1,768,768]{4,3,2,1,0:T(8,128)} %param.13) | copy-start | bytes 7077892
  40.8 96.1 %copy-start.12 = (f32[6,6,128]{2,1,0:T(8,128)}, f32[6,6,128]{2,1,0:T(8,128)S(1)}, u32[]{:S(2)}) copy-start(f32[6,6,128]{2,1,0:T(8,128)S(1)} %fusion.16) | copy-start | bytes 55300
  41.6 21.3 %collective-permute-start = (f32[1,128,128]{2,1,0:T(8,128)S(1)}, f32[1,128,128]{2,1,0:T(8,128)}, u32[]{:S(2)}, u32[]{:S(2)}) collective-permute-start(f32[1,128,128]{2,1,0:T(8,128)S(1)} %slice.456), channel_id=1, source_target_pairs={{0,16},{16,0},{1,17},{17,1},{2,18},{18,2},{3,19},{19,3},{4,20},{20... | collective-permute-start | bytes 196616 | tf_op jit(solution)/shard_map/ppermute | solution.py:20
  63.7 11.6 %collective-permute-start.1 = (f32[1,128,128]{2,1,0:T(8,128)S(1)}, f32[1,128,128]{2,1,0:T(8,128)}, u32[]{:S(2)}, u32[]{:S(2)}) collective-permute-start(f32[1,128,128]{2,1,0:T(8,128)S(1)} %get-tuple-element.63), channel_id=1, source_target_pairs={{16,0},{0,16},{17,1},{1,17},{18,2},{2,18},{19,3},{3,19},{20,4},{4,... | collective-permute-start | bytes 196616 | tf_op jit(solution)/shard_map/ppermute | solution.py:21
  70.7 7.4 collective-permute-start.5
  70.7 7.3 collective-permute-start.4
  71.2 6.8 collective-permute-start.2
  71.2 6.8 collective-permute-start.3
  78.8 57.9 %copy-start.36 = (f32[1,1,1,6,192]{4,2,3,1,0:T(1,128)S(1)}, f32[1,1,1,6,192]{4,2,3,1,0:T(1,128)}, u32[]{:S(2)}) copy-start(f32[1,1,1,6,192]{4,2,3,1,0:T(1,128)} %param.17) | copy-start | bytes 13828
  82.5 4.3 collective-permute-start.6
  86.9 11.1 %collective-permute-start.11 = (f32[1,128,128]{2,1,0:T(8,128)S(1)}, f32[1,128,128]{2,1,0:T(8,128)S(1)}, u32[]{:S(2)}, u32[]{:S(2)}) collective-permute-start(f32[1,128,128]{2,1,0:T(8,128)S(1)} %get-tuple-element.52), channel_id=1, source_target_pairs={{1,0},{2,1},{3,2},{0,3},{5,4},{6,5},{7,6},{4,7},{9,8},{10,9},{11,1... | collective-permute-start | bytes 196616 | tf_op jit(solution)/shard_map/ppermute | solution.py:21
  87.0 11.0 %collective-permute-start.10 = (f32[1,128,128]{2,1,0:T(8,128)S(1)}, f32[1,128,128]{2,1,0:T(8,128)S(1)}, u32[]{:S(2)}, u32[]{:S(2)}) collective-permute-start(f32[1,128,128]{2,1,0:T(8,128)S(1)} %get-tuple-element.54), channel_id=1, source_target_pairs={{0,1},{1,2},{2,3},{3,0},{4,5},{5,6},{6,7},{7,4},{8,9},{9,10},{10,1... | collective-permute-start | bytes 196616 | tf_op jit(solution)/shard_map/ppermute | solution.py:20
  87.5 8.9 %collective-permute-start.8 = (f32[1,128,128]{2,1,0:T(8,128)S(1)}, f32[1,128,128]{2,1,0:T(8,128)S(1)}, u32[]{:S(2)}, u32[]{:S(2)}) collective-permute-start(f32[1,128,128]{2,1,0:T(8,128)S(1)} %get-tuple-element.55), channel_id=1, source_target_pairs={{0,4},{4,8},{8,12},{12,0},{1,5},{5,9},{9,13},{13,1},{2,6},{6,10},{... | collective-permute-start | bytes 196616 | tf_op jit(solution)/shard_map/ppermute | solution.py:20
  92.1 5.9 collective-permute-start.9
  92.1 4.3 collective-permute-start.7
  137.7 77.5 %copy-start.87 = (f32[40]{0:T(128)S(1)}, f32[40]{0:T(128)}, u32[]{:S(2)}) copy-start(f32[40]{0:T(128)} %param.20) | copy-start | bytes 484
  137.7 4.4 collective-permute-start.12
  142.2 9.3 %collective-permute-start.17 = (f32[1,128,128]{2,1,0:T(8,128)S(1)}, f32[1,128,128]{2,1,0:T(8,128)S(1)}, u32[]{:S(2)}, u32[]{:S(2)}) collective-permute-start(f32[1,128,128]{2,1,0:T(8,128)S(1)} %get-tuple-element.46), channel_id=1, source_target_pairs={{1,0},{2,1},{3,2},{0,3},{5,4},{6,5},{7,6},{4,7},{9,8},{10,9},{11,1... | collective-permute-start | bytes 196616 | tf_op jit(solution)/shard_map/ppermute | solution.py:21
  142.2 9.2 %collective-permute-start.16 = (f32[1,128,128]{2,1,0:T(8,128)S(1)}, f32[1,128,128]{2,1,0:T(8,128)S(1)}, u32[]{:S(2)}, u32[]{:S(2)}) collective-permute-start(f32[1,128,128]{2,1,0:T(8,128)S(1)} %get-tuple-element.48), channel_id=1, source_target_pairs={{0,1},{1,2},{2,3},{3,0},{4,5},{5,6},{6,7},{7,4},{8,9},{9,10},{10,1... | collective-permute-start | bytes 196616 | tf_op jit(solution)/shard_map/ppermute | solution.py:20
  142.7 8.6 %collective-permute-start.14 = (f32[1,128,128]{2,1,0:T(8,128)S(1)}, f32[1,128,128]{2,1,0:T(8,128)S(1)}, u32[]{:S(2)}, u32[]{:S(2)}) collective-permute-start(f32[1,128,128]{2,1,0:T(8,128)S(1)} %get-tuple-element.49), channel_id=1, source_target_pairs={{0,4},{4,8},{8,12},{12,0},{1,5},{5,9},{9,13},{13,1},{2,6},{6,10},{... | collective-permute-start | bytes 196616 | tf_op jit(solution)/shard_map/ppermute | solution.py:20
  142.7 8.7 %collective-permute-start.15 = (f32[1,128,128]{2,1,0:T(8,128)S(1)}, f32[1,128,128]{2,1,0:T(8,128)S(1)}, u32[]{:S(2)}, u32[]{:S(2)}) collective-permute-start(f32[1,128,128]{2,1,0:T(8,128)S(1)} %get-tuple-element.50), channel_id=1, source_target_pairs={{4,0},{8,4},{12,8},{0,12},{5,1},{9,5},{13,9},{1,13},{6,2},{10,6},{... | collective-permute-start | bytes 196616 | tf_op jit(solution)/shard_map/ppermute | solution.py:21
  146.9 4.4 collective-permute-start.13
  217.0 23.1 %copy-start.13 = (f32[6,6,128]{2,1,0:T(8,128)S(1)}, f32[6,6,128]{2,1,0:T(8,128)}, u32[]{:S(2)}) copy-start(f32[6,6,128]{2,1,0:T(8,128)} %copy-done.12) | copy-start | bytes 55300
  220.8 5.9 collective-permute-start.18
  226.6 13.4 %collective-permute-start.23 = (f32[1,128,128]{2,1,0:T(8,128)S(1)}, f32[1,128,128]{2,1,0:T(8,128)S(1)}, u32[]{:S(2)}, u32[]{:S(2)}) collective-permute-start(f32[1,128,128]{2,1,0:T(8,128)S(1)} %get-tuple-element.40), channel_id=1, source_target_pairs={{1,0},{2,1},{3,2},{0,3},{5,4},{6,5},{7,6},{4,7},{9,8},{10,9},{11,1... | collective-permute-start | bytes 196616 | tf_op jit(solution)/shard_map/ppermute | solution.py:21
  226.7 13.3 %collective-permute-start.22 = (f32[1,128,128]{2,1,0:T(8,128)S(1)}, f32[1,128,128]{2,1,0:T(8,128)S(1)}, u32[]{:S(2)}, u32[]{:S(2)}) collective-permute-start(f32[1,128,128]{2,1,0:T(8,128)S(1)} %get-tuple-element.42), channel_id=1, source_target_pairs={{0,1},{1,2},{2,3},{3,0},{4,5},{5,6},{6,7},{7,4},{8,9},{9,10},{10,1... | collective-permute-start | bytes 196616 | tf_op jit(solution)/shard_map/ppermute | solution.py:20
  227.2 12.7 %collective-permute-start.20 = (f32[1,128,128]{2,1,0:T(8,128)S(1)}, f32[1,128,128]{2,1,0:T(8,128)S(1)}, u32[]{:S(2)}, u32[]{:S(2)}) collective-permute-start(f32[1,128,128]{2,1,0:T(8,128)S(1)} %get-tuple-element.43), channel_id=1, source_target_pairs={{0,4},{4,8},{8,12},{12,0},{1,5},{5,9},{9,13},{13,1},{2,6},{6,10},{... | collective-permute-start | bytes 196616 | tf_op jit(solution)/shard_map/ppermute | solution.py:20
  227.2 12.8 %collective-permute-start.21 = (f32[1,128,128]{2,1,0:T(8,128)S(1)}, f32[1,128,128]{2,1,0:T(8,128)S(1)}, u32[]{:S(2)}, u32[]{:S(2)}) collective-permute-start(f32[1,128,128]{2,1,0:T(8,128)S(1)} %get-tuple-element.44), channel_id=1, source_target_pairs={{4,0},{8,4},{12,8},{0,12},{5,1},{9,5},{13,9},{1,13},{6,2},{10,6},{... | collective-permute-start | bytes 196616 | tf_op jit(solution)/shard_map/ppermute | solution.py:21
  235.7 4.3 collective-permute-start.19
  283.9 7.8 %collective-permute-start.24 = (f32[1,128,128]{2,1,0:T(8,128)S(1)}, f32[1,128,128]{2,1,0:T(8,128)S(1)}, u32[]{:S(2)}, u32[]{:S(2)}) collective-permute-start(f32[1,128,128]{2,1,0:T(8,128)S(1)} %slice.480), channel_id=1, source_target_pairs={{0,16},{16,0},{1,17},{17,1},{2,18},{18,2},{3,19},{19,3},{4,20},{20... | collective-permute-start | bytes 196616 | tf_op jit(solution)/shard_map/ppermute | solution.py:20
  291.7 10.4 %collective-permute-start.29 = (f32[1,128,128]{2,1,0:T(8,128)S(1)}, f32[1,128,128]{2,1,0:T(8,128)S(1)}, u32[]{:S(2)}, u32[]{:S(2)}) collective-permute-start(f32[1,128,128]{2,1,0:T(8,128)S(1)} %get-tuple-element.34), channel_id=1, source_target_pairs={{1,0},{2,1},{3,2},{0,3},{5,4},{6,5},{7,6},{4,7},{9,8},{10,9},{11,1... | collective-permute-start | bytes 196616 | tf_op jit(solution)/shard_map/ppermute | solution.py:21
  293.5 8.5 %collective-permute-start.28 = (f32[1,128,128]{2,1,0:T(8,128)S(1)}, f32[1,128,128]{2,1,0:T(8,128)S(1)}, u32[]{:S(2)}, u32[]{:S(2)}) collective-permute-start(f32[1,128,128]{2,1,0:T(8,128)S(1)} %get-tuple-element.36), channel_id=1, source_target_pairs={{0,1},{1,2},{2,3},{3,0},{4,5},{5,6},{6,7},{7,4},{8,9},{9,10},{10,1... | collective-permute-start | bytes 196616 | tf_op jit(solution)/shard_map/ppermute | solution.py:20
  293.5 8.4 %collective-permute-start.26 = (f32[1,128,128]{2,1,0:T(8,128)S(1)}, f32[1,128,128]{2,1,0:T(8,128)S(1)}, u32[]{:S(2)}, u32[]{:S(2)}) collective-permute-start(f32[1,128,128]{2,1,0:T(8,128)S(1)} %get-tuple-element.37), channel_id=1, source_target_pairs={{0,4},{4,8},{8,12},{12,0},{1,5},{5,9},{9,13},{13,1},{2,6},{6,10},{... | collective-permute-start | bytes 196616 | tf_op jit(solution)/shard_map/ppermute | solution.py:20
  293.5 8.5 %collective-permute-start.27 = (f32[1,128,128]{2,1,0:T(8,128)S(1)}, f32[1,128,128]{2,1,0:T(8,128)S(1)}, u32[]{:S(2)}, u32[]{:S(2)}) collective-permute-start(f32[1,128,128]{2,1,0:T(8,128)S(1)} %get-tuple-element.38), channel_id=1, source_target_pairs={{4,0},{8,4},{12,8},{0,12},{5,1},{9,5},{13,9},{1,13},{6,2},{10,6},{... | collective-permute-start | bytes 196616 | tf_op jit(solution)/shard_map/ppermute | solution.py:21
  297.7 4.3 collective-permute-start.25
  415.6 4.3 collective-permute-start.30
  420.0 13.4 %collective-permute-start.35 = (f32[1,128,128]{2,1,0:T(8,128)S(1)}, f32[1,128,128]{2,1,0:T(8,128)S(1)}, u32[]{:S(2)}, u32[]{:S(2)}) collective-permute-start(f32[1,128,128]{2,1,0:T(8,128)S(1)} %get-tuple-element.28), channel_id=1, source_target_pairs={{1,0},{2,1},{3,2},{0,3},{5,4},{6,5},{7,6},{4,7},{9,8},{10,9},{11,1... | collective-permute-start | bytes 196616 | tf_op jit(solution)/shard_map/ppermute | solution.py:21
  420.1 13.3 %collective-permute-start.34 = (f32[1,128,128]{2,1,0:T(8,128)S(1)}, f32[1,128,128]{2,1,0:T(8,128)S(1)}, u32[]{:S(2)}, u32[]{:S(2)}) collective-permute-start(f32[1,128,128]{2,1,0:T(8,128)S(1)} %get-tuple-element.30), channel_id=1, source_target_pairs={{0,1},{1,2},{2,3},{3,0},{4,5},{5,6},{6,7},{7,4},{8,9},{9,10},{10,1... | collective-permute-start | bytes 196616 | tf_op jit(solution)/shard_map/ppermute | solution.py:20
  420.6 12.7 %collective-permute-start.32 = (f32[1,128,128]{2,1,0:T(8,128)S(1)}, f32[1,128,128]{2,1,0:T(8,128)S(1)}, u32[]{:S(2)}, u32[]{:S(2)}) collective-permute-start(f32[1,128,128]{2,1,0:T(8,128)S(1)} %get-tuple-element.31), channel_id=1, source_target_pairs={{0,4},{4,8},{8,12},{12,0},{1,5},{5,9},{9,13},{13,1},{2,6},{6,10},{... | collective-permute-start | bytes 196616 | tf_op jit(solution)/shard_map/ppermute | solution.py:20
  420.6 12.8 %collective-permute-start.33 = (f32[1,128,128]{2,1,0:T(8,128)S(1)}, f32[1,128,128]{2,1,0:T(8,128)S(1)}, u32[]{:S(2)}, u32[]{:S(2)}) collective-permute-start(f32[1,128,128]{2,1,0:T(8,128)S(1)} %get-tuple-element.32), channel_id=1, source_target_pairs={{4,0},{8,4},{12,8},{0,12},{5,1},{9,5},{13,9},{1,13},{6,2},{10,6},{... | collective-permute-start | bytes 196616 | tf_op jit(solution)/shard_map/ppermute | solution.py:21
  429.0 4.3 collective-permute-start.31
  470.8 21.7 %copy-start.20 = (f32[6,128,128]{2,1,0:T(8,128)S(1)}, f32[6,128,128]{2,1,0:T(8,128)}, u32[]{:S(2)}) copy-start(f32[6,128,128]{2,1,0:T(8,128)} %copy-done.19) | copy-start | bytes 1179652
  472.6 8.4 %collective-permute-start.36 = (f32[1,128,128]{2,1,0:T(8,128)S(1)}, f32[1,128,128]{2,1,0:T(8,128)S(1)}, u32[]{:S(2)}, u32[]{:S(2)}) collective-permute-start(f32[1,128,128]{2,1,0:T(8,128)S(1)} %slice.494), channel_id=1, source_target_pairs={{0,16},{16,0},{1,17},{17,1},{2,18},{18,2},{3,19},{19,3},{4,20},{20... | collective-permute-start | bytes 196616 | tf_op jit(solution)/shard_map/ppermute | solution.py:20
  481.0 10.3 %collective-permute-start.41 = (f32[1,128,128]{2,1,0:T(8,128)S(1)}, f32[1,128,128]{2,1,0:T(8,128)S(1)}, u32[]{:S(2)}, u32[]{:S(2)}) collective-permute-start(f32[1,128,128]{2,1,0:T(8,128)S(1)} %get-tuple-element.22), channel_id=1, source_target_pairs={{1,0},{2,1},{3,2},{0,3},{5,4},{6,5},{7,6},{4,7},{9,8},{10,9},{11,1... | collective-permute-start | bytes 196616 | tf_op jit(solution)/shard_map/ppermute | solution.py:21
  482.7 8.5 %collective-permute-start.40 = (f32[1,128,128]{2,1,0:T(8,128)S(1)}, f32[1,128,128]{2,1,0:T(8,128)S(1)}, u32[]{:S(2)}, u32[]{:S(2)}) collective-permute-start(f32[1,128,128]{2,1,0:T(8,128)S(1)} %get-tuple-element.24), channel_id=1, source_target_pairs={{0,1},{1,2},{2,3},{3,0},{4,5},{5,6},{6,7},{7,4},{8,9},{9,10},{10,1... | collective-permute-start | bytes 196616 | tf_op jit(solution)/shard_map/ppermute | solution.py:20
  482.7 8.4 %collective-permute-start.38 = (f32[1,128,128]{2,1,0:T(8,128)S(1)}, f32[1,128,128]{2,1,0:T(8,128)S(1)}, u32[]{:S(2)}, u32[]{:S(2)}) collective-permute-start(f32[1,128,128]{2,1,0:T(8,128)S(1)} %get-tuple-element.25), channel_id=1, source_target_pairs={{0,4},{4,8},{8,12},{12,0},{1,5},{5,9},{9,13},{13,1},{2,6},{6,10},{... | collective-permute-start | bytes 196616 | tf_op jit(solution)/shard_map/ppermute | solution.py:20
  482.7 8.5 %collective-permute-start.39 = (f32[1,128,128]{2,1,0:T(8,128)S(1)}, f32[1,128,128]{2,1,0:T(8,128)S(1)}, u32[]{:S(2)}, u32[]{:S(2)}) collective-permute-start(f32[1,128,128]{2,1,0:T(8,128)S(1)} %get-tuple-element.26), channel_id=1, source_target_pairs={{4,0},{8,4},{12,8},{0,12},{5,1},{9,5},{13,9},{1,13},{6,2},{10,6},{... | collective-permute-start | bytes 196616 | tf_op jit(solution)/shard_map/ppermute | solution.py:21
  486.9 4.3 collective-permute-start.37
  606.1 4.3 collective-permute-start.42
  610.4 13.4 %collective-permute-start.47 = (f32[1,128,128]{2,1,0:T(8,128)S(1)}, f32[1,128,128]{2,1,0:T(8,128)S(1)}, u32[]{:S(2)}, u32[]{:S(2)}) collective-permute-start(f32[1,128,128]{2,1,0:T(8,128)S(1)} %get-tuple-element.16), channel_id=1, source_target_pairs={{1,0},{2,1},{3,2},{0,3},{5,4},{6,5},{7,6},{4,7},{9,8},{10,9},{11,1... | collective-permute-start | bytes 196616 | tf_op jit(solution)/shard_map/ppermute | solution.py:21
  610.5 13.3 %collective-permute-start.46 = (f32[1,128,128]{2,1,0:T(8,128)S(1)}, f32[1,128,128]{2,1,0:T(8,128)S(1)}, u32[]{:S(2)}, u32[]{:S(2)}) collective-permute-start(f32[1,128,128]{2,1,0:T(8,128)S(1)} %get-tuple-element.18), channel_id=1, source_target_pairs={{0,1},{1,2},{2,3},{3,0},{4,5},{5,6},{6,7},{7,4},{8,9},{9,10},{10,1... | collective-permute-start | bytes 196616 | tf_op jit(solution)/shard_map/ppermute | solution.py:20
  611.0 12.7 %collective-permute-start.44 = (f32[1,128,128]{2,1,0:T(8,128)S(1)}, f32[1,128,128]{2,1,0:T(8,128)S(1)}, u32[]{:S(2)}, u32[]{:S(2)}) collective-permute-start(f32[1,128,128]{2,1,0:T(8,128)S(1)} %get-tuple-element.19), channel_id=1, source_target_pairs={{0,4},{4,8},{8,12},{12,0},{1,5},{5,9},{9,13},{13,1},{2,6},{6,10},{... | collective-permute-start | bytes 196616 | tf_op jit(solution)/shard_map/ppermute | solution.py:20
  611.0 12.8 %collective-permute-start.45 = (f32[1,128,128]{2,1,0:T(8,128)S(1)}, f32[1,128,128]{2,1,0:T(8,128)S(1)}, u32[]{:S(2)}, u32[]{:S(2)}) collective-permute-start(f32[1,128,128]{2,1,0:T(8,128)S(1)} %get-tuple-element.20), channel_id=1, source_target_pairs={{4,0},{8,4},{12,8},{0,12},{5,1},{9,5},{13,9},{1,13},{6,2},{10,6},{... | collective-permute-start | bytes 196616 | tf_op jit(solution)/shard_map/ppermute | solution.py:21
  619.5 4.3 collective-permute-start.43
  661.0 21.8 %copy-start.22 = (f32[6,128,128]{2,1,0:T(8,128)S(1)}, f32[6,128,128]{2,1,0:T(8,128)}, u32[]{:S(2)}) copy-start(f32[6,128,128]{2,1,0:T(8,128)} %copy-done.21) | copy-start | bytes 1179652
  662.8 63.2 %copy-start.10 = (f32[6,128,128]{2,1,0:T(8,128)S(1)}, f32[6,128,128]{2,1,0:T(8,128)}, u32[]{:S(2)}) copy-start(f32[6,128,128]{2,1,0:T(8,128)} %get-tuple-element.69) | copy-start | bytes 1179652
  662.9 63.2 %copy-start.89 = (f32[128]{0:T(128)S(1)}, f32[128]{0:T(128)}, u32[]{:S(2)}) copy-start(f32[128]{0:T(128)} %copy-done.88) | copy-start | bytes 1540
  662.9 63.2 %copy-start.91 = (f32[128]{0:T(128)S(1)}, f32[128]{0:T(128)}, u32[]{:S(2)}) copy-start(f32[128]{0:T(128)} %copy-done.90) | copy-start | bytes 1540
  662.9 8.4 %collective-permute-start.48 = (f32[1,128,128]{2,1,0:T(8,128)S(1)}, f32[1,128,128]{2,1,0:T(8,128)S(1)}, u32[]{:S(2)}, u32[]{:S(2)}) collective-permute-start(f32[1,128,128]{2,1,0:T(8,128)S(1)} %slice.509), channel_id=1, source_target_pairs={{0,16},{16,0},{1,17},{17,1},{2,18},{18,2},{3,19},{19,3},{4,20},{20... | collective-permute-start | bytes 196616 | tf_op jit(solution)/shard_map/ppermute | solution.py:20
  671.3 10.3 %collective-permute-start.53 = (f32[1,128,128]{2,1,0:T(8,128)S(1)}, f32[1,128,128]{2,1,0:T(8,128)S(1)}, u32[]{:S(2)}, u32[]{:S(2)}) collective-permute-start(f32[1,128,128]{2,1,0:T(8,128)S(1)} %get-tuple-element.10), channel_id=1, source_target_pairs={{1,0},{2,1},{3,2},{0,3},{5,4},{6,5},{7,6},{4,7},{9,8},{10,9},{11,1... | collective-permute-start | bytes 196616 | tf_op jit(solution)/shard_map/ppermute | solution.py:21
  673.0 8.5 %collective-permute-start.52 = (f32[1,128,128]{2,1,0:T(8,128)S(1)}, f32[1,128,128]{2,1,0:T(8,128)S(1)}, u32[]{:S(2)}, u32[]{:S(2)}) collective-permute-start(f32[1,128,128]{2,1,0:T(8,128)S(1)} %get-tuple-element.12), channel_id=1, source_target_pairs={{0,1},{1,2},{2,3},{3,0},{4,5},{5,6},{6,7},{7,4},{8,9},{9,10},{10,1... | collective-permute-start | bytes 196616 | tf_op jit(solution)/shard_map/ppermute | solution.py:20
  673.0 8.4 %collective-permute-start.50 = (f32[1,128,128]{2,1,0:T(8,128)S(1)}, f32[1,128,128]{2,1,0:T(8,128)S(1)}, u32[]{:S(2)}, u32[]{:S(2)}) collective-permute-start(f32[1,128,128]{2,1,0:T(8,128)S(1)} %get-tuple-element.13), channel_id=1, source_target_pairs={{0,4},{4,8},{8,12},{12,0},{1,5},{5,9},{9,13},{13,1},{2,6},{6,10},{... | collective-permute-start | bytes 196616 | tf_op jit(solution)/shard_map/ppermute | solution.py:20
  673.0 8.5 %collective-permute-start.51 = (f32[1,128,128]{2,1,0:T(8,128)S(1)}, f32[1,128,128]{2,1,0:T(8,128)S(1)}, u32[]{:S(2)}, u32[]{:S(2)}) collective-permute-start(f32[1,128,128]{2,1,0:T(8,128)S(1)} %get-tuple-element.14), channel_id=1, source_target_pairs={{4,0},{8,4},{12,8},{0,12},{5,1},{9,5},{13,9},{1,13},{6,2},{10,6},{... | collective-permute-start | bytes 196616 | tf_op jit(solution)/shard_map/ppermute | solution.py:21
  677.2 4.3 collective-permute-start.49
  (83 other events, 478.9 us)
